TPU v7x, 32 devices: a whole 2x2x4 slice. The times are simulated.
32 devices in a mesh: expert: 16 (over z, y, x), tok: 2 (over core).
Axes of the slice: x: 2, y: 2, z: 4, core: 2. Of those that a mesh axis runs over, the one named last changes fastest.
Arguments:
- tokens: bfloat16 [2048, 3584], P(('expert', 'tok')), may hold values from -6 to 6
- routes: int32 [2048, 8], P(('expert', 'tok')), may hold values from 0 to 15, all different within a row; in each aligned block of 64 rows (0 to 63, 64 to 127, ...) at most 36 rows name the same one
- gates: float32 [2048, 8], P(('expert', 'tok')), may hold values from 0.05 to 1
- upstream: bfloat16 [2048, 3584], P(('expert', 'tok')), may hold values from -6 to 6
- w_up: bfloat16 [16, 3584, 1024], P('expert', None, 'tok'), may hold values from -0.09375 to 0.09375
- w_down: bfloat16 [16, 1024, 3584], P('expert', 'tok'), may hold values from -0.1875 to 0.1875
Outputs:
- mixed: bfloat16 [2048, 3584], P(('expert', 'tok'))
- d_tokens: bfloat16 [2048, 3584], P(('expert', 'tok'))
- d_gates: float32 [2048, 8], P(('expert', 'tok'))
- grad_up: bfloat16 [16, 3584, 1024], P('expert', None, 'tok')
- grad_down: bfloat16 [16, 1024, 3584], P('expert', 'tok')
Inputs may be any that keep to these rules, and one draw needn't show every extreme that they name: `routes`: each token names 8 different experts. At most 36 of the 64 tokens of one device name the same expert, and in every draw the tokens of some device name some expert exactly 36 times.
All inputs are finite; a program needn't handle non-finite values.
Results may differ from a plain program's by a relative error of at most 0.0065.
Values may be sent and summed in bfloat16 or wider, within the bound.
A program may use at most 192 MiB of HBM per device.

v0:
```python
import jax
import jax.numpy as jnp
from jax import lax
from jax.sharding import PartitionSpec as P

GELU_C = 0.7978845608028654
GELU_A = 0.044715


def gelu_value(hidden):
    inner_arg = GELU_C * (hidden + GELU_A * hidden * hidden * hidden)
    return 0.5 * hidden * (1.0 + jnp.tanh(inner_arg))


def gelu_slope(hidden):
    tangent = jnp.tanh(GELU_C * (hidden + GELU_A * hidden * hidden * hidden))
    return 0.5 * (1.0 + tangent) + 0.5 * hidden * (1.0 - tangent * tangent) * GELU_C * (
        1.0 + 3.0 * GELU_A * hidden * hidden
    )


def expert_rows(rows_x, rows_grad, up_local, down_local):
    hidden = jnp.dot(rows_x, up_local, preferred_element_type=jnp.float32)
    active = gelu_value(hidden).astype(jnp.bfloat16)
    out_part = jnp.dot(active, down_local, preferred_element_type=jnp.float32)
    d_active = lax.dot_general(
        rows_grad, down_local, (((1,), (1,)), ((), ())), preferred_element_type=jnp.float32
    )
    d_hidden = (d_active * gelu_slope(hidden)).astype(jnp.bfloat16)
    dx_part = lax.dot_general(
        d_hidden, up_local, (((1,), (1,)), ((), ())), preferred_element_type=jnp.float32
    )
    grad_down = lax.dot_general(
        active, rows_grad, (((0,), (0,)), ((), ())), preferred_element_type=jnp.float32
    )
    grad_up = lax.dot_general(
        rows_x, d_hidden, (((0,), (0,)), ((), ())), preferred_element_type=jnp.float32
    )
    return (out_part, dx_part, grad_up, grad_down)


def routed_shards(tokens, routes, gates, upstream, w_up, w_down):
    tok_rows, feature_width = tokens.shape
    top_count = routes.shape[1]
    owners = lax.axis_size("expert")
    pair_count = lax.axis_size("tok")
    capacity = tok_rows * top_count // owners + max(1, tok_rows * top_count // (8 * owners))
    assigned = routes.reshape(-1)
    labels = jnp.arange(owners, dtype=jnp.int32)
    onehot = (assigned[:, None] == labels[None, :]).astype(jnp.int32)
    earlier = jnp.cumsum(onehot, axis=0) - onehot
    slot_rank = jnp.sum(earlier * onehot, axis=1)
    slot_of = assigned * capacity + slot_rank
    slot_ids = jnp.arange(owners * capacity, dtype=jnp.int32)
    matches = (slot_of[None, :] == slot_ids[:, None]).astype(jnp.int32)
    filled = jnp.sum(matches, axis=1) > 0
    source = jnp.sum(matches * jnp.arange(assigned.shape[0], dtype=jnp.int32)[None, :], axis=1)
    token_ids = source // top_count
    send_x = jnp.where(filled[:, None], tokens[token_ids], jnp.zeros((), jnp.bfloat16))
    gate_rows = jnp.where(filled, gates.reshape(-1)[source], jnp.zeros((), jnp.float32))
    send_grad = (gate_rows[:, None] * upstream[token_ids].astype(jnp.float32)).astype(jnp.bfloat16)
    send_x = send_x.reshape(owners, capacity, feature_width)
    send_grad = send_grad.reshape(owners, capacity, feature_width)
    recv_x, recv_grad = (
        lax.all_to_all(send_x, "expert", split_axis=0, concat_axis=0, tiled=True),
        lax.all_to_all(send_grad, "expert", split_axis=0, concat_axis=0, tiled=True),
    )
    both_x, both_grad = (
        lax.all_gather(recv_x[None], "tok", axis=0, tiled=True),
        lax.all_gather(recv_grad[None], "tok", axis=0, tiled=True),
    )
    rows_x = both_x.reshape(-1, feature_width)
    rows_grad = both_grad.reshape(-1, feature_width)
    out_part, dx_part, grad_up, grad_down = expert_rows(rows_x, rows_grad, w_up[0], w_down[0])
    shaped_out = out_part.reshape(pair_count, owners, capacity, feature_width)
    shaped_dx = dx_part.reshape(pair_count, owners, capacity, feature_width)
    summed_out, summed_dx = (
        lax.psum_scatter(shaped_out, "tok", scatter_dimension=0, tiled=True),
        lax.psum_scatter(shaped_dx, "tok", scatter_dimension=0, tiled=True),
    )
    home_out, home_dx = (
        lax.all_to_all(
            summed_out[0].astype(jnp.bfloat16), "expert", split_axis=0, concat_axis=0, tiled=True
        ),
        lax.all_to_all(
            summed_dx[0].astype(jnp.bfloat16), "expert", split_axis=0, concat_axis=0, tiled=True
        ),
    )
    out_pairs = (
        home_out.reshape(owners * capacity, feature_width)[slot_of]
        .reshape(tok_rows, top_count, feature_width)
        .astype(jnp.float32)
    )
    dx_pairs = (
        home_dx.reshape(owners * capacity, feature_width)[slot_of]
        .reshape(tok_rows, top_count, feature_width)
        .astype(jnp.float32)
    )
    mixed_out = jnp.sum(gates[:, :, None] * out_pairs, axis=1).astype(jnp.bfloat16)
    d_gates = jnp.sum(upstream.astype(jnp.float32)[:, None, :] * out_pairs, axis=2)
    d_tokens = jnp.sum(dx_pairs, axis=1).astype(jnp.bfloat16)
    return (
        mixed_out,
        d_tokens,
        d_gates,
        grad_up.astype(jnp.bfloat16)[None],
        grad_down.astype(jnp.bfloat16)[None],
    )


def dense_shards(tokens, routes, gates, upstream, w_up, w_down):
    tok_rows, width = tokens.shape
    owners = lax.axis_size("expert")
    half = w_up.shape[2]
    swap = ((0, 1), (1, 0))
    up_local, down_local = (w_up[0], w_down[0])
    up_full = jnp.concatenate([up_local, lax.ppermute(up_local, "tok", swap)], axis=1)
    down_full = jnp.concatenate([down_local, lax.ppermute(down_local, "tok", swap)], axis=0)
    named = routes[:, :, None] == jnp.arange(owners, dtype=jnp.int32)
    gate_of = jnp.sum(jnp.where(named, gates[:, :, None], 0.0), axis=1)
    gate = lax.all_to_all(gate_of.T, "expert", split_axis=0, concat_axis=0, tiled=True)
    gate = gate.reshape(-1)[:, None]
    all_x = lax.all_gather(tokens, "expert", axis=0, tiled=True)
    all_u = lax.all_gather(upstream, "expert", axis=0, tiled=True)
    hidden = jnp.dot(all_x, up_full, preferred_element_type=jnp.float32)
    gated = (gate * gelu_value(hidden)).astype(jnp.bfloat16)
    mixed_part = jnp.dot(gated, down_full, preferred_element_type=jnp.float32)
    mixed = lax.psum_scatter(
        mixed_part.astype(jnp.bfloat16), "expert", scatter_dimension=0, tiled=True
    )
    back = lax.dot_general(
        all_u, down_full, (((1,), (1,)), ((), ())), preferred_element_type=jnp.float32
    )
    inner = jnp.sum(gelu_value(hidden) * back, axis=1)
    d_hidden = (gate * back * gelu_slope(hidden)).astype(jnp.bfloat16)
    dx_part = lax.dot_general(
        d_hidden, up_full, (((1,), (1,)), ((), ())), preferred_element_type=jnp.float32
    )
    d_tokens = lax.psum_scatter(
        dx_part.astype(jnp.bfloat16), "expert", scatter_dimension=0, tiled=True
    )
    home = lax.all_to_all(
        inner.reshape(owners, tok_rows), "expert", split_axis=0, concat_axis=0, tiled=True
    )
    d_gates = jnp.sum(jnp.where(named, home.T[:, None, :], 0.0), axis=2)

    def outer(rows, columns):
        return lax.dot_general(
            rows, columns, (((0,), (0,)), ((), ())), preferred_element_type=jnp.float32
        )

    down_far = outer(gated[:, half:], all_u).astype(jnp.bfloat16)
    up_far = outer(all_x, d_hidden[:, half:]).astype(jnp.bfloat16)
    down_near = outer(gated[:, :half], all_u)
    up_near = outer(all_x, d_hidden[:, :half])
    grad_down = down_near + lax.ppermute(down_far, "tok", swap).astype(jnp.float32)
    grad_up = up_near + lax.ppermute(up_far, "tok", swap).astype(jnp.float32)
    return (
        mixed,
        d_tokens,
        d_gates,
        grad_up.astype(jnp.bfloat16)[None],
        grad_down.astype(jnp.bfloat16)[None],
    )


def shards(tokens, routes, gates, upstream, w_up, w_down):
    dense = 2 * routes.shape[1] >= lax.axis_size("expert") and lax.axis_size("tok") == 2
    body = dense_shards if dense else routed_shards
    return body(tokens, routes, gates, upstream, w_up, w_down)


def solution(mesh):
    return jax.shard_map(
        shards,
        mesh=mesh,
        in_specs=(
            P(("expert", "tok"), None),
            P(("expert", "tok"), None),
            P(("expert", "tok"), None),
            P(("expert", "tok"), None),
            P("expert", None, "tok"),
            P("expert", "tok", None),
        ),
        out_specs=(
            P(("expert", "tok"), None),
            P(("expert", "tok"), None),
            P(("expert", "tok"), None),
            P("expert", None, "tok"),
            P("expert", "tok", None),
        ),
        check_vma=False,
    )
```

profile of v0, /device:TPU:10, one launch (start us, length us, event | category | flops | bytes accessed | tf_op | source)
XLA Modules:
  0.0 600.3 jit_solution(6524580034297987019)
XLA Ops:
  7.2 0.7 all-gather.3.cloned.1.call-update
  7.9 0.7 all-gather.5.cloned.1.call-update
  8.8 0.5 collective-permute-start.1
  9.3 6.2 %collective-permute-done = bf16[3584,512]{1,0:T(8,128)(2,1)} collective-permute-done((bf16[3584,512]{1,0:T(8,128)(2,1)}, bf16[3584,512]{1,0:T(8,128)(2,1)}, u32[]{:S(2)}, u32[]{:S(2)}) %collective-permute-start) | collective-permute-done | bytes 3670048 | tf_op jit(solution)/shard_map/ppermute | solution.py:117
  15.5 98.8 %all-gather.3.cloned.1.call-done = bf16[1024,3584]{1,0:T(8,128)(2,1)} async-done(((bf16[64,3584]{1,0:T(8,128)(2,1)}), bf16[1024,3584]{1,0:T(8,128)(2,1)}) %all-gather.3.cloned.1.call-update) | async-done | bytes 7340048 | tf_op jit(solution)/shard_map/all_gather | solution.py:123
  114.3 13.6 %fusion.4 = f32[1024,1024]{1,0:T(8,128)} fusion(bf16[1024,3584]{1,0:T(8,128)(2,1)} %all-gather.3.cloned.1.call-done, bf16[3584,512]{1,0:T(8,128)(2,1)} %collective-permute-done, bf16[3584,512]{1,0:T(8,128)(2,1)} %bitcast.60), kind=kOutput, calls=%fused_computation.14 | convolution fusion | flops 7530872832 | bytes 18874368 | tf_op jit(solution)/shard_map/dot_general | solution.py:125
  127.9 90.8 %all-gather.5.cloned.1.call-done = bf16[1024,3584]{1,0:T(8,128)(2,1)} async-done(((bf16[64,3584]{1,0:T(8,128)(2,1)}), bf16[1024,3584]{1,0:T(8,128)(2,1)}) %all-gather.5.cloned.1.call-update) | async-done | bytes 7340048 | tf_op jit(solution)/shard_map/all_gather | solution.py:124
  218.7 15.0 %fusion.12 = (f32[1024]{0:T(1024)S(1)}, f32[1024,1024]{1,0:T(8,128)}) fusion(f32[1024,1024]{1,0:T(8,128)} %fusion.4, bf16[1024,3584]{1,0:T(8,128)(2,1)} %all-gather.5.cloned.1.call-done, bf16[512,3584]{1,0:T(8,128)(2,1)} %collective-permute-done.1, bf16[512,3584]{1,0:T(8,128)(2,1)} %bitcast.63), kind=kOutput, calls=%fused_computation.24 | convolution fusion | flops 7541357568 | bytes 23072768 | tf_op jit(solution)/shard_map/dot_general | solution.py:131
  233.7 10.0 %all_to_all.21 = f32[16,1,64]{2,1,0:T(1,128)S(1)} all-to-all(f32[16,1,64]{2,1,0:T(1,128)S(1)} %bitcast.56), channel_id=1, replica_groups=mesh['expert'=16,'tok'=2] {'expert'}, dimensions={0} | all-to-all | bytes 8192 | tf_op jit(solution)/shard_map/all_to_all | solution.py:142
  243.8 0.6 select_reduce_fusion
  244.4 9.8 %all_to_all.22 = f32[16,1,64]{2,1,0:T(1,128)S(1)} all-to-all(f32[16,1,64]{2,1,0:T(1,128)S(1)} %bitcast.55), channel_id=1, replica_groups=mesh['expert'=16,'tok'=2] {'expert'}, dimensions={0} | all-to-all | bytes 8192 | tf_op jit(solution)/shard_map/all_to_all | solution.py:121
  254.2 0.5 broadcast.46
  254.7 0.7 reduce.3
  255.5 5.6 fusion.11
  261.1 1.3 copy-done
  262.4 12.0 %convolution_convert_fusion = bf16[1024,3584]{1,0:T(8,128)(2,1)} fusion(bf16[1024,1024]{0,1:T(8,128)(2,1)S(1)} %get-tuple-element.27, bf16[3584,512]{1,0:T(8,128)(2,1)} %collective-permute-done, bf16[3584,512]{1,0:T(8,128)(2,1)S(1)} %bitcast.61), kind=kOutput, calls=%fused_computation | convolution fusion | flops 7534542848 | bytes 16777216 | tf_op jit(solution)/shard_map/dot_general | solution.py:136
  274.6 13.0 %convolution_convert_fusion.1 = bf16[1024,3584]{1,0:T(8,128)(2,1)} fusion(bf16[1024,1024]{0,1:T(8,128)(2,1)S(1)} %get-tuple-element.28, bf16[512,3584]{1,0:T(8,128)(2,1)} %collective-permute-done.1, bf16[512,3584]{1,0:T(8,128)(2,1)} %bitcast.64), kind=kOutput, calls=%fused_computation.1 | convolution fusion | flops 7534542848 | bytes 16777216 | tf_op jit(solution)/shard_map/dot_general | solution.py:127
  287.7 7.5 %fusion.1 = bf16[3584,512]{0,1:T(8,128)(2,1)S(1)} fusion(bf16[1024,3584]{1,0:T(8,128)(2,1)} %all-gather.3.cloned.1.call-done, bf16[1024,1024]{0,1:T(8,128)(2,1)} %copy-done), kind=kOutput, calls=%fused_computation.11 | convolution fusion | flops 3759931392 | bytes 12058624 | tf_op jit(solution)/shard_map/dot_general | solution.py:148
  295.4 8.7 %convolution_convert_fusion.2 = bf16[512,3584]{1,0:T(8,128)(2,1)} fusion(bf16[1024,3584]{1,0:T(8,128)(2,1)} %all-gather.5.cloned.1.call-done, bf16[1024,1024]{0,1:T(8,128)(2,1)S(1)} %get-tuple-element.28), kind=kOutput, calls=%fused_computation.9 | convolution fusion | flops 3759931392 | bytes 12058624 | tf_op jit(solution)/shard_map/dot_general | solution.py:148
  304.4 5.4 fusion.2
  309.8 5.9 copy.25
  315.7 9.1 %fusion.14 = bf16[1,512,3584]{2,1,0:T(8,128)(2,1)} fusion(bf16[512,3584]{1,0:T(8,128)(2,1)} %collective-permute-done.3, bf16[1024,3584]{1,0:T(8,128)(2,1)} %all-gather.5.cloned.1.call-done, bf16[1024,1024]{0,1:T(8,128)(2,1)S(1)} %get-tuple-element.28), kind=kOutput, calls=%fused_computation.28 | convolution fusion | flops 3763601408 | bytes 15728640 | tf_op jit(solution)/shard_map/dot_general | solution.py:148
  324.8 107.0 %reduce-scatter.5.cloned.1.call-done = bf16[64,3584]{1,0:T(8,128)(2,1)} async-done(((bf16[1024,3584]{1,0:T(8,128)(2,1)}), bf16[64,3584]{1,0:T(8,128)(2,1)}) %reduce-scatter.5.cloned.1.call-update) | async-done | bytes 458768 | tf_op jit(solution)/shard_map/reduce_scatter | solution.py:139
  431.8 161.9 %reduce-scatter.3.cloned.1.call-done = bf16[64,3584]{1,0:T(8,128)(2,1)} async-done(((bf16[1024,3584]{1,0:T(8,128)(2,1)}), bf16[64,3584]{1,0:T(8,128)(2,1)}) %reduce-scatter.3.cloned.1.call-update) | async-done | bytes 458768 | tf_op jit(solution)/shard_map/reduce_scatter | solution.py:128
  (28 shorter events, 1.0 us)
Async XLA Ops:
  7.2 107.2 %all-gather.3.cloned.1.call-start = ((), (), s32[]{:S(2)}) async-start(), calls=%async_computation.4 | async-start | bytes 7798784 | tf_op jit(solution)/shard_map/all_gather | solution.py:123
  7.9 210.8 %all-gather.5.cloned.1.call-start = ((), (), s32[]{:S(2)}) async-start(), calls=%async_computation.6 | async-start | bytes 7798784 | tf_op jit(solution)/shard_map/all_gather | solution.py:124
  8.6 423.2 %reduce-scatter.5.cloned.1.call-start = ((), (), s32[]{:S(2)}) async-start(), calls=%async_computation.7 | async-start | bytes 7798784 | tf_op jit(solution)/shard_map/reduce_scatter | solution.py:139
  8.7 6.8 %collective-permute-start = (bf16[3584,512]{1,0:T(8,128)(2,1)}, bf16[3584,512]{1,0:T(8,128)(2,1)}, u32[]{:S(2)}, u32[]{:S(2)}) collective-permute-start(bf16[3584,512]{1,0:T(8,128)(2,1)} %bitcast.59), channel_id=1, source_target_pairs={{0,1},{1,0},{2,3},{3,2},{4,5},{5,4},{6,7},{7,6},{8,9},{9,8},{10,11... | collective-permute-start | bytes 11010056 | tf_op jit(solution)/shard_map/ppermute | solution.py:117
  8.8 119.1 %collective-permute-start.1 = (bf16[512,3584]{1,0:T(8,128)(2,1)}, bf16[512,3584]{1,0:T(8,128)(2,1)}, u32[]{:S(2)}, u32[]{:S(2)}) collective-permute-start(bf16[512,3584]{1,0:T(8,128)(2,1)} %bitcast.62), channel_id=1, source_target_pairs={{0,1},{1,0},{2,3},{3,2},{4,5},{5,4},{6,7},{7,6},{8,9},{9,8},{10,11... | collective-permute-start | bytes 11010056 | tf_op jit(solution)/shard_map/ppermute | solution.py:118
  127.9 115.9 %copy-start.2 = (s32[64,8]{0,1:T(8,128)S(1)}, s32[64,8]{0,1:T(8,128)}, u32[]{:S(2)}) copy-start(s32[64,8]{0,1:T(8,128)} %param.7) | copy-start | bytes 6148
  127.9 115.9 %copy-start.3 = (f32[64,8]{0,1:T(8,128)S(1)}, f32[64,8]{0,1:T(8,128)}, u32[]{:S(2)}) copy-start(f32[64,8]{0,1:T(8,128)} %param.8) | copy-start | bytes 6148
  255.5 6.9 %copy-start.4 = (bf16[1,3584,512]{2,1,0:T(8,128)(2,1)S(1)}, bf16[1,3584,512]{2,1,0:T(8,128)(2,1)}, u32[]{:S(2)}) copy-start(bf16[1,3584,512]{2,1,0:T(8,128)(2,1)} %param.10) | copy-start | bytes 11010052
  261.1 1.3 copy-start
  274.4 319.4 %reduce-scatter.3.cloned.1.call-start = ((), (), s32[]{:S(2)}) async-start(), calls=%async_computation.5 | async-start | bytes 7798784 | tf_op jit(solution)/shard_map/reduce_scatter | solution.py:128
  287.7 16.6 %slice-start = ((s8[7340032]{0:T(1024)(128)(4,1)}), s8[4194304]{0:T(1024)(128)(4,1)S(1)}, s32[]{:S(2)}) async-start(s8[7340032]{0:T(1024)(128)(4,1)} %bitcast.57), calls=%async_computation.8 | async-start | bytes 8388608
  295.3 9.1 %copy-start.1 = (bf16[1024,1024]{0,1:T(8,128)(2,1)S(1)}, bf16[1024,1024]{0,1:T(8,128)(2,1)}, u32[]{:S(2)}) copy-start(bf16[1024,1024]{0,1:T(8,128)(2,1)} %copy-done) | copy-start | bytes 6291460
  295.3 9.1 %slice-start.1 = ((s8[7340032]{0:T(1024)(128)(4,1)}), s8[3145728]{0:T(1024)(128)(4,1)S(1)}, s32[]{:S(2)}) async-start(s8[7340032]{0:T(1024)(128)(4,1)} %bitcast.57), calls=%async_computation.9 | async-start | bytes 6291456
  295.3 9.1 %collective-permute-start.2 = (bf16[3584,512]{0,1:T(8,128)(2,1)S(1)}, bf16[3584,512]{0,1:T(8,128)(2,1)S(1)}, u32[]{:S(2)}, u32[]{:S(2)}) collective-permute-start(bf16[3584,512]{0,1:T(8,128)(2,1)S(1)} %fusion.1), channel_id=1, source_target_pairs={{0,1},{1,0},{2,3},{3,2},{4,5},{5,4},{6,7},{7,6},{8,9},{9,8},{10,11... | collective-permute-start | bytes 11010056 | tf_op jit(solution)/shard_map/ppermute | solution.py:157
  304.0 11.7 %collective-permute-start.3 = (bf16[512,3584]{1,0:T(8,128)(2,1)}, bf16[512,3584]{1,0:T(8,128)(2,1)}, u32[]{:S(2)}, u32[]{:S(2)}) collective-permute-start(bf16[512,3584]{1,0:T(8,128)(2,1)} %convolution_convert_fusion.2), channel_id=1, source_target_pairs={{0,1},{1,0},{2,3},{3,2},{4,5},{5,4},{6,7},{7,6},{8,9},{9,8},{10,11... | collective-permute-start | bytes 11010056 | tf_op jit(solution)/shard_map/ppermute | solution.py:156
Sparse Core Ops, SparseCore 0:
  10.7 103.6 all-gather.2
  117.0 101.6 all-gather.4
  274.5 157.2 reduce-scatter.4
  434.6 159.1 reduce-scatter.2
where the time goes:
time: 601 us; the launch traced here: 600 us
  waiting for transfers between devices  466 us (78%)
  matrix products  84.3 us (14%)
  blocking collectives  19.9 us (3%)
  between operations  13.9 us (2%)
  local copies, waits for them, and re-layouts  7.92 us (1%)
  other arithmetic  6.87 us (1%)
    reduce_scatter x1, waiting for transfers between devices, dense_shards(): lax.psum_scatter(mixed_part.astype(jnp.bfloat16), 'expert', scatter_dimen...  162 us
    reduce_scatter x1, waiting for transfers between devices, dense_shards(): lax.psum_scatter(dx_part.astype(jnp.bfloat16), 'expert', scatter_dimensio...  107 us
    all_gather x1, waiting for transfers between devices, dense_shards(): all_x = lax.all_gather(tokens, 'expert', axis=0, tiled=True)  98.8 us
    all_gather x1, waiting for transfers between devices, dense_shards(): all_u = lax.all_gather(upstream, 'expert', axis=0, tiled=True)  90.8 us
    dot_general x4, matrix products, outer(): lax.dot_general(rows, columns, (((0,), (0,)), ((), ())), preferred_elemen...  30.7 us
    dot_general x1, matrix products, dense_shards(): lax.dot_general(all_u, down_full, (((1,), (1,)), ((), ())), preferred_ele...  15 us
    dot_general x1, matrix products, dense_shards(): hidden = jnp.dot(all_x, up_full, preferred_element_type=jnp.float32)  13.6 us
    dot_general x1, matrix products, dense_shards(): mixed_part = jnp.dot(gated, down_full, preferred_element_type=jnp.float32)  13 us
  transfers between devices with their start and end apart: 8, of which 5 were waited for; matrix products, arithmetic and copies ran while one was open for 11% of the time, Pallas kernels for 0%

commit v1 on v0

--- a/solution.py
+++ b/solution.py
@@ -120,8 +120,15 @@
     gate_of = jnp.sum(jnp.where(named, gates[:, :, None], 0.0), axis=1)
     gate = lax.all_to_all(gate_of.T, "expert", split_axis=0, concat_axis=0, tiled=True)
     gate = gate.reshape(-1)[:, None]
-    all_x = lax.all_gather(tokens, "expert", axis=0, tiled=True)
-    all_u = lax.all_gather(upstream, "expert", axis=0, tiled=True)
+
+    def _lay_scenes(shard_in, patch):
+        return jnp.split(
+            lax.all_gather(jnp.concatenate([shard_in, patch], 1), "expert", axis=0, tiled=True),
+            [shard_in.shape[1]],
+            axis=1,
+        )
+
+    all_x, all_u = _lay_scenes(tokens, upstream)
     hidden = jnp.dot(all_x, up_full, preferred_element_type=jnp.float32)
     gated = (gate * gelu_value(hidden)).astype(jnp.bfloat16)
     mixed_part = jnp.dot(gated, down_full, preferred_element_type=jnp.float32)

time: 601 us -> 580 us (0.965)
  waiting for transfers between devices: 466 us -> 448 us
  local copies, waits for them, and re-layouts: 7.92 us -> 0.69 us
    reduce_scatter x1, waiting for transfers between devices: 107 us -> 162 us  [dense_shards(): lax.psum_scatter(dx_part.astype(jnp.bfloat16), 'expert', scatter_dimensio...]
    reduce_scatter x1, waiting for transfers between devices: 162 us -> 113 us  [dense_shards(): lax.psum_scatter(mixed_part.astype(jnp.bfloat16), 'expert', scatter_dimen...]
    all_gather x2 -> x1, waiting for transfers between devices: 190 us -> 166 us  [_lay_scenes(): lax.all_gather(jnp.concatenate([shard_in, patch], 1), 'expert', axis=0, t...]
    unnamed x15 -> x18, local copies, waits for them, and re-layouts: 7.26 us -> 0.04 us
  transfers between devices with their start and end apart: 8 -> 7, of which waited for: 5 -> 4; matrix products, arithmetic and copies ran while one was open for 11% -> 10% of each run, Pallas kernels for 0% -> 0%
where the time goes in v1:
time: 580 us; the launch traced here: 579 us
  waiting for transfers between devices  448 us (77%)
  matrix products  85 us (15%)
  blocking collectives  20.9 us (4%)
  between operations  13.9 us (2%)
  other arithmetic  9.96 us (2%)
    all_gather x1, waiting for transfers between devices, _lay_scenes(): lax.all_gather(jnp.concatenate([shard_in, patch], 1), 'expert', axis=0, t...  166 us
    reduce_scatter x1, waiting for transfers between devices, dense_shards(): lax.psum_scatter(dx_part.astype(jnp.bfloat16), 'expert', scatter_dimensio...  162 us
    reduce_scatter x1, waiting for transfers between devices, dense_shards(): lax.psum_scatter(mixed_part.astype(jnp.bfloat16), 'expert', scatter_dimen...  113 us
    dot_general x4, matrix products, outer(): lax.dot_general(rows, columns, (((0,), (0,)), ((), ())), preferred_elemen...  30.9 us
    dot_general x1, matrix products, dense_shards(): lax.dot_general(all_u, down_full, (((1,), (1,)), ((), ())), preferred_ele...  17.1 us
    dot_general x1, matrix products, dense_shards(): lax.dot_general(d_hidden, up_full, (((1,), (1,)), ((), ())), preferred_el...  12.6 us
    dot_general x1, matrix products, dense_shards(): hidden = jnp.dot(all_x, up_full, preferred_element_type=jnp.float32)  12.2 us
    dot_general x1, matrix products, dense_shards(): mixed_part = jnp.dot(gated, down_full, preferred_element_type=jnp.float32)  12.1 us
  transfers between devices with their start and end apart: 7, of which 4 were waited for; matrix products, arithmetic and copies ran while one was open for 10% of the time, Pallas kernels for 0%

profile of v1, /device:TPU:10, one launch (start us, length us, event | category | flops | bytes accessed | tf_op | source)
XLA Modules:
  0.0 579.4 jit_solution(14672776238427808939)
XLA Ops:
  7.2 2.1 pad_maximum_fusion.6
  9.4 0.1 collective-permute-start
  9.5 0.5 collective-permute-start.1
  10.0 6.2 %collective-permute-done = bf16[3584,512]{1,0:T(8,128)(2,1)} collective-permute-done((bf16[3584,512]{1,0:T(8,128)(2,1)}, bf16[3584,512]{1,0:T(8,128)(2,1)}, u32[]{:S(2)}, u32[]{:S(2)}) %collective-permute-start) | collective-permute-done | bytes 3670048 | tf_op jit(solution)/shard_map/ppermute | solution.py:117
  16.2 166.1 %all-gather.2.cloned.1.call-done = bf16[1024,7168]{1,0:T(8,128)(2,1)} async-done(((bf16[64,7168]{1,0:T(8,128)(2,1)}), bf16[1024,7168]{1,0:T(8,128)(2,1)}) %all-gather.2.cloned.1.call-update) | async-done | bytes 14680080 | tf_op jit(solution)/shard_map/all_gather | solution.py:126
  182.3 12.2 %fusion.10 = f32[1024,1024]{0,1:T(8,128)S(1)} fusion(bf16[1024,7168]{1,0:T(8,128)(2,1)} %all-gather.2.cloned.1.call-done, bf16[3584,512]{1,0:T(8,128)(2,1)} %collective-permute-done, bf16[3584,512]{1,0:T(8,128)(2,1)} %bitcast.26), kind=kOutput, calls=%fused_computation.18 | convolution fusion | flops 7530872832 | bytes 18874368 | tf_op jit(solution)/shard_map/dot_general | solution.py:132
  194.6 17.1 %multiply_reduce_fusion = (f32[1024]{0:T(1024)S(1)}, f32[1024,1024]{0,1:T(8,128)}) fusion(f32[1024,1024]{0,1:T(8,128)S(1)} %fusion.10, bf16[512,3584]{1,0:T(8,128)(2,1)} %collective-permute-done.1, bf16[512,3584]{1,0:T(8,128)(2,1)} %bitcast.23, bf16[1024,7168]{1,0:T(8,128)(2,1)} %all-gather.2.cloned.1.call-done), kind=kOutput, calls=%fused_computation.29 | convolution fusion | flops 7541357568 | bytes 23072768 | tf_op jit(solution)/shard_map/dot_general | solution.py:138
  211.7 0.1 all_to_all.16
  211.8 11.1 %all_to_all.21 = f32[16,1,64]{2,1,0:T(1,128)S(1)} all-to-all(f32[16,1,64]{2,1,0:T(1,128)S(1)} %bitcast.19), channel_id=1, replica_groups=mesh['expert'=16,'tok'=2] {'expert'}, dimensions={0} | all-to-all | bytes 8192 | tf_op jit(solution)/shard_map/all_to_all | solution.py:149
  222.9 0.6 select_reduce_fusion
  223.5 9.8 %all_to_all.22 = f32[16,1,64]{2,1,0:T(1,128)S(1)} all-to-all(f32[16,1,64]{2,1,0:T(1,128)S(1)} %bitcast.18), channel_id=1, replica_groups=mesh['expert'=16,'tok'=2] {'expert'}, dimensions={0} | all-to-all | bytes 8192 | tf_op jit(solution)/shard_map/all_to_all | solution.py:121
  233.4 0.5 broadcast.46
  233.9 0.7 reduce.3
  234.5 0.1 mul.75
  234.6 6.5 %fusion.26 = (bf16[1024,1024]{0,1:T(8,128)(2,1)}, bf16[1024,1024]{0,1:T(8,128)(2,1)S(1)}) fusion(f32[1024,1024]{0,1:T(8,128)} %copy-done, f32[1024,1024]{0,1:T(8,128)} %get-tuple-element.10, f32[1024]{0:T(1024)S(1)} %mul.75), kind=kLoop, calls=%fused_computation.28 | loop fusion | flops 24117248 | bytes 12587008 | tf_op jit(solution)/shard_map/convert_element_type | solution.py:142
  241.1 12.1 %convolution_convert_fusion.1 = bf16[1024,3584]{1,0:T(8,128)(2,1)} fusion(bf16[1024,1024]{0,1:T(8,128)(2,1)S(1)} %get-tuple-element.8, bf16[512,3584]{1,0:T(8,128)(2,1)} %collective-permute-done.1, bf16[512,3584]{1,0:T(8,128)(2,1)S(1)} %bitcast.24), kind=kOutput, calls=%fused_computation.1 | convolution fusion | flops 7534542848 | bytes 16777216 | tf_op jit(solution)/shard_map/dot_general | solution.py:134
  253.4 12.6 %convolution_convert_fusion = bf16[1024,3584]{1,0:T(8,128)(2,1)} fusion(bf16[1024,1024]{0,1:T(8,128)(2,1)} %get-tuple-element.7, bf16[3584,512]{1,0:T(8,128)(2,1)} %collective-permute-done, bf16[3584,512]{1,0:T(8,128)(2,1)} %bitcast.27), kind=kOutput, calls=%fused_computation | convolution fusion | flops 7534542848 | bytes 16777216 | tf_op jit(solution)/shard_map/dot_general | solution.py:143
  266.0 9.4 %convolution_convert_fusion.3 = bf16[3584,512]{1,0:T(8,128)(2,1)} fusion(bf16[1024,7168]{1,0:T(8,128)(2,1)} %all-gather.2.cloned.1.call-done, bf16[1024,1024]{0,1:T(8,128)(2,1)} %get-tuple-element.7), kind=kOutput, calls=%fused_computation.9 | convolution fusion | flops 3759931392 | bytes 12058624 | tf_op jit(solution)/shard_map/dot_general | solution.py:155
  275.4 8.6 %convolution_convert_fusion.2 = bf16[512,3584]{1,0:T(8,128)(2,1)} fusion(bf16[1024,7168]{1,0:T(8,128)(2,1)} %all-gather.2.cloned.1.call-done, bf16[1024,1024]{0,1:T(8,128)(2,1)S(1)} %get-tuple-element.8), kind=kOutput, calls=%fused_computation.8 | convolution fusion | flops 3759931392 | bytes 12058624 | tf_op jit(solution)/shard_map/dot_general | solution.py:155
  284.1 0.3 collective-permute-start.3
  284.5 7.4 %fusion.14 = bf16[1,3584,512]{2,1,0:T(8,128)(2,1)} fusion(bf16[3584,512]{1,0:T(8,128)(2,1)} %collective-permute-done.2, bf16[1024,7168]{1,0:T(8,128)(2,1)S(1)} %bitcast.21, bf16[1024,1024]{0,1:T(8,128)(2,1)S(1)} %copy-done.1), kind=kOutput, calls=%fused_computation.20 | convolution fusion | flops 3763601408 | bytes 15728640 | tf_op jit(solution)/shard_map/dot_general | solution.py:155
  291.9 5.5 fusion.17
  297.4 113.4 %reduce-scatter.3.cloned.1.call-done = bf16[64,3584]{1,0:T(8,128)(2,1)} async-done(((bf16[1024,3584]{1,0:T(8,128)(2,1)}), bf16[64,3584]{1,0:T(8,128)(2,1)}) %reduce-scatter.3.cloned.1.call-update) | async-done | bytes 458768 | tf_op jit(solution)/shard_map/reduce_scatter | solution.py:135
  410.8 162.0 %reduce-scatter.5.cloned.1.call-done = bf16[64,3584]{1,0:T(8,128)(2,1)} async-done(((bf16[1024,3584]{1,0:T(8,128)(2,1)}), bf16[64,3584]{1,0:T(8,128)(2,1)}) %reduce-scatter.5.cloned.1.call-update) | async-done | bytes 458768 | tf_op jit(solution)/shard_map/reduce_scatter | solution.py:146
  (29 shorter events, 0.2 us)
Async XLA Ops:
  7.2 175.2 %all-gather.2.cloned.1.call-start = ((), (), s32[]{:S(2)}) async-start(), calls=%async_computation.4 | async-start | bytes 15597568 | tf_op jit(solution)/shard_map/all_gather | solution.py:126
  9.4 401.4 %reduce-scatter.3.cloned.1.call-start = ((), (), s32[]{:S(2)}) async-start(), calls=%async_computation.5 | async-start | bytes 7798784 | tf_op jit(solution)/shard_map/reduce_scatter | solution.py:135
  9.4 6.8 %collective-permute-start = (bf16[3584,512]{1,0:T(8,128)(2,1)}, bf16[3584,512]{1,0:T(8,128)(2,1)}, u32[]{:S(2)}, u32[]{:S(2)}) collective-permute-start(bf16[3584,512]{1,0:T(8,128)(2,1)} %bitcast.25), channel_id=1, source_target_pairs={{0,1},{1,0},{2,3},{3,2},{4,5},{5,4},{6,7},{7,6},{8,9},{9,8},{10,11... | collective-permute-start | bytes 11010056 | tf_op jit(solution)/shard_map/ppermute | solution.py:117
  9.5 185.1 %collective-permute-start.1 = (bf16[512,3584]{1,0:T(8,128)(2,1)}, bf16[512,3584]{1,0:T(8,128)(2,1)}, u32[]{:S(2)}, u32[]{:S(2)}) collective-permute-start(bf16[512,3584]{1,0:T(8,128)(2,1)} %bitcast.22), channel_id=1, source_target_pairs={{0,1},{1,0},{2,3},{3,2},{4,5},{5,4},{6,7},{7,6},{8,9},{9,8},{10,11... | collective-permute-start | bytes 11010056 | tf_op jit(solution)/shard_map/ppermute | solution.py:118
  194.6 17.1 %copy-start = (f32[1024,1024]{0,1:T(8,128)}, f32[1024,1024]{0,1:T(8,128)S(1)}, u32[]{:S(2)}) copy-start(f32[1024,1024]{0,1:T(8,128)S(1)} %fusion.10) | copy-start | bytes 12582916
  194.6 28.3 %copy-start.2 = (s32[64,8]{0,1:T(8,128)S(1)}, s32[64,8]{0,1:T(8,128)}, u32[]{:S(2)}) copy-start(s32[64,8]{0,1:T(8,128)} %param.7) | copy-start | bytes 6148
  194.6 28.3 %copy-start.3 = (f32[64,8]{0,1:T(8,128)S(1)}, f32[64,8]{0,1:T(8,128)}, u32[]{:S(2)}) copy-start(f32[64,8]{0,1:T(8,128)} %param.8) | copy-start | bytes 6148
  234.6 6.5 %copy-start.4 = (bf16[1,512,3584]{2,1,0:T(8,128)(2,1)S(1)}, bf16[1,512,3584]{2,1,0:T(8,128)(2,1)}, u32[]{:S(2)}) copy-start(bf16[1,512,3584]{2,1,0:T(8,128)(2,1)} %param.11) | copy-start | bytes 11010052
  253.3 319.5 %reduce-scatter.5.cloned.1.call-start = ((), (), s32[]{:S(2)}) async-start(), calls=%async_computation.6 | async-start | bytes 7798784 | tf_op jit(solution)/shard_map/reduce_scatter | solution.py:146
  266.0 18.4 %slice-start = ((s8[14680064]{0:T(1024)(128)(4,1)}), s8[4194304]{0:T(1024)(128)(4,1)S(1)}, s32[]{:S(2)}) async-start(s8[14680064]{0:T(1024)(128)(4,1)} %bitcast.20), calls=%async_computation.7 | async-start | bytes 8388608
  266.0 18.4 %slice-start.1 = ((s8[14680064]{0:T(1024)(128)(4,1)}), s8[4194304]{0:T(1024)(128)(4,1)S(1)}, s32[]{:S(2)}) async-start(s8[14680064]{0:T(1024)(128)(4,1)} %bitcast.20), calls=%async_computation.8 | async-start | bytes 8388608
  275.4 9.0 %copy-start.1 = (bf16[1024,1024]{0,1:T(8,128)(2,1)S(1)}, bf16[1024,1024]{0,1:T(8,128)(2,1)}, u32[]{:S(2)}) copy-start(bf16[1024,1024]{0,1:T(8,128)(2,1)} %get-tuple-element.7) | copy-start | bytes 6291460
  275.4 9.0 %slice-start.2 = ((s8[14680064]{0:T(1024)(128)(4,1)}), s8[4194304]{0:T(1024)(128)(4,1)S(1)}, s32[]{:S(2)}) async-start(s8[14680064]{0:T(1024)(128)(4,1)} %bitcast.20), calls=%async_computation.9 | async-start | bytes 8388608
  275.4 9.0 %slice-start.3 = ((s8[14680064]{0:T(1024)(128)(4,1)}), s8[2097152]{0:T(1024)(128)(4,1)S(1)}, s32[]{:S(2)}) async-start(s8[14680064]{0:T(1024)(128)(4,1)} %bitcast.20), calls=%async_computation.10 | async-start | bytes 4194304
  275.4 9.0 %collective-permute-start.2 = (bf16[3584,512]{1,0:T(8,128)(2,1)}, bf16[3584,512]{1,0:T(8,128)(2,1)}, u32[]{:S(2)}, u32[]{:S(2)}) collective-permute-start(bf16[3584,512]{1,0:T(8,128)(2,1)} %convolution_convert_fusion.3), channel_id=1, source_target_pairs={{0,1},{1,0},{2,3},{3,2},{4,5},{5,4},{6,7},{7,6},{8,9},{9,8},{10,11... | collective-permute-start | bytes 11010056 | tf_op jit(solution)/shard_map/ppermute | solution.py:164
  284.1 7.8 %collective-permute-start.3 = (bf16[512,3584]{1,0:T(8,128)(2,1)}, bf16[512,3584]{1,0:T(8,128)(2,1)S(1)}, u32[]{:S(2)}, u32[]{:S(2)}) collective-permute-start(bf16[512,3584]{1,0:T(8,128)(2,1)} %convolution_convert_fusion.2), channel_id=1, source_target_pairs={{0,1},{1,0},{2,3},{3,2},{4,5},{5,4},{6,7},{7,6},{8,9},{9,8},{10,11... | collective-permute-start | bytes 11010056 | tf_op jit(solution)/shard_map/ppermute | solution.py:163
Sparse Core Ops, SparseCore 0:
  11.3 170.9 all-gather.1
  253.4 157.3 reduce-scatter.2
  413.7 159.1 reduce-scatter.4
